TPU v7x, 256 devices: a whole 4x4x8 slice. The times are simulated.
256 devices in a mesh: prow: 16 (over z, core), pcol: 16 (over y, x).
Axes of the slice: x: 4, y: 4, z: 8, core: 2. Of those that a mesh axis runs over, the one named last changes fastest.
Arguments:
- root_inverse: float32 [2, 16, 128, 2, 16, 128], P(None, 'prow', None, None, 'pcol'), as said below
- lower_one: float32 [2, 16, 128, 1, 16, 128], P(None, 'prow', None, None, 'pcol'), may hold values from -0.125 to 0.125
- lower_two: float32 [3, 16, 128, 1, 16, 128], P(None, 'prow', None, None, 'pcol'), may hold values from -0.15625 to 0.15625
- dinv_one: float32 [1, 16, 128, 1, 16, 128], P(None, 'prow', None, None, 'pcol'), as said below
- dinv_two: float32 [1, 16, 128, 1, 16, 128], P(None, 'prow', None, None, 'pcol'), as said below
- seg_one: int32 [16], replicated, may hold values from 0 to 2, as said below
- seg_two: int32 [16], replicated, may hold values from 0 to 3, as said below
- parent_two: int32 [4], replicated, may hold values from 0 to 2
- pattern_one: int32 [3, 32], replicated, may hold values 0 or 1
- pattern_two: int32 [4, 48], replicated, may hold values 0 or 1
Outputs:
- inverse_one: float32 [1, 16, 128, 1, 16, 128], P(None, 'prow', None, None, 'pcol')
- inverse_two: float32 [1, 16, 128, 1, 16, 128], P(None, 'prow', None, None, 'pcol')
Inputs may be any that keep to these rules, and one draw needn't show every extreme that they name: `root_inverse`: Block-diagonal over supernodes is not implied; this is a symmetric matrix. `dinv_one`: Symmetric, and zero in every block whose row and column blocks belong to different supernodes of seg_one. `dinv_two`: Symmetric, and zero in every block whose row and column blocks belong to different supernodes of seg_two. `seg_one`: never falls; every supernode 0 to 2 has 1 to 8 consecutive blocks, one exactly 8. `seg_two`: never falls; every supernode 0 to 3 has 1 to 8 consecutive blocks, one exactly 8.
All inputs are finite; a program needn't handle non-finite values.
Results may differ from a plain program's by a relative error of at most 0.00005.
Values sent between devices are 32-bit elements; how exact they have to be, the bound alone decides.
A program may use at most 64 MiB of HBM per device.

v0:
```python
import jax
import jax.numpy as jnp
from jax import lax
from jax.sharding import PartitionSpec as P

highest = lax.Precision.HIGHEST


def contract(left_side, right_side):
    return lax.dot_general(
        left_side,
        right_side,
        (((0,), (0,)), ((), ())),
        precision=highest,
        preferred_element_type=jnp.float32,
    )


def flatten_local(blocks):
    squeezed = blocks[:, 0, :, :, 0, :]
    return squeezed.reshape(
        squeezed.shape[0] * squeezed.shape[1], squeezed.shape[2] * squeezed.shape[3]
    )


def to_blocks(matrix, block_width):
    return matrix.reshape(
        matrix.shape[0] // block_width,
        1,
        block_width,
        matrix.shape[1] // block_width,
        1,
        block_width,
    )


def apply_mask(matrix, block_mask, block_width):
    row_blocks = block_mask.shape[0]
    col_blocks = block_mask.shape[1]
    shaped = matrix.reshape(row_blocks, block_width, col_blocks, block_width)
    return (shaped * block_mask[:, None, :, None]).reshape(
        row_blocks * block_width, col_blocks * block_width
    )


def split_rows(matrix, pieces, block_width):
    return matrix.reshape(
        matrix.shape[0] // (pieces * block_width), pieces, block_width, matrix.shape[1]
    )


def merge_rows(blocks):
    return blocks.reshape(blocks.shape[0] * blocks.shape[1] * blocks.shape[2], blocks.shape[3])


def row_panel(gathered):
    picked = gathered[:, 0]
    return picked.reshape(
        picked.shape[0] * picked.shape[1], picked.shape[2] * picked.shape[3] * picked.shape[4]
    )


def same_mask(first_ids, second_ids):
    return (first_ids[:, None] == second_ids[None, :]).astype(jnp.float32)


def on_device(
    root_inverse,
    lower_one,
    lower_two,
    dinv_one,
    dinv_two,
    seg_one,
    seg_two,
    parent_two,
    pattern_one,
    pattern_two,
):
    block_width = root_inverse.shape[2]
    prow_total = lax.axis_size("prow")
    pcol_total = lax.axis_size("pcol")
    prow_place = lax.axis_index("prow")
    pcol_place = lax.axis_index("pcol")
    root_blocks = pattern_one.shape[1]
    first_nodes = pattern_one.shape[0]
    second_nodes = pattern_two.shape[0]

    def row_ids(amount):
        return jnp.arange(amount, dtype=jnp.int32) * prow_total + prow_place

    def col_ids(amount):
        return jnp.arange(amount, dtype=jnp.int32) * pcol_total + pcol_place

    root_rows = row_ids(root_inverse.shape[0])
    first_cols = col_ids(lower_one.shape[3])
    seg_cols = seg_one[first_cols]
    pick_first = same_mask(seg_cols, jnp.arange(first_nodes, dtype=jnp.int32))
    mask_one = jnp.dot(pick_first, pattern_one[:, root_rows].astype(jnp.float32)).T
    masked_one = apply_mask(flatten_local(lower_one), mask_one, block_width)
    second_rows = row_ids(lower_two.shape[0])
    second_cols = col_ids(lower_two.shape[3])
    seg_two_cols = seg_two[second_cols]
    parent_cols = parent_two[seg_two_cols]
    pick_second = same_mask(seg_two_cols, jnp.arange(second_nodes, dtype=jnp.int32))
    own_pattern = jnp.dot(pick_second, pattern_two[:, second_rows].astype(jnp.float32))
    pick_parent = same_mask(parent_cols, jnp.arange(first_nodes, dtype=jnp.int32))
    root_reach = jnp.dot(
        pick_parent, pattern_one[:, jnp.minimum(second_rows, root_blocks - 1)].astype(jnp.float32)
    )
    level_index = jnp.clip(second_rows - root_blocks, 0, seg_one.shape[0] - 1)
    level_reach = (seg_one[level_index][None, :] == parent_cols[:, None]).astype(jnp.float32)
    reachable = jnp.where((second_rows < root_blocks)[None, :], root_reach, level_reach)
    mask_two = (own_pattern * reachable).T
    masked_two = apply_mask(flatten_local(lower_two), mask_two, block_width)
    root_local = flatten_local(root_inverse)
    root_gathered, first_gathered, second_gathered = (
        lax.all_gather(root_inverse, "pcol", axis=4, tiled=True),
        lax.all_gather(to_blocks(masked_one, block_width), "pcol", axis=4, tiled=True),
        lax.all_gather(to_blocks(masked_two, block_width), "pcol", axis=4, tiled=True),
    )
    root_full = row_panel(root_gathered)
    first_full = row_panel(first_gathered)
    second_full = row_panel(second_gathered)
    turned_part = split_rows(contract(first_full, root_local), prow_total, block_width)
    solved_part = split_rows(contract(root_full, masked_one), prow_total, block_width)
    solved_blocks, turned_blocks = (
        lax.psum_scatter(solved_part, "prow", scatter_dimension=1, tiled=True),
        lax.psum_scatter(turned_part, "prow", scatter_dimension=1, tiled=True),
    )
    solved_one = merge_rows(solved_blocks)
    turned_one = merge_rows(turned_blocks)
    diag_part = split_rows(contract(first_full, solved_one), prow_total, block_width)
    diag_one = merge_rows(lax.psum_scatter(diag_part, "prow", scatter_dimension=1, tiled=True))
    same_one = same_mask(seg_one[row_ids(dinv_one.shape[0])], seg_one[col_ids(dinv_one.shape[3])])
    inverse_one = apply_mask(flatten_local(dinv_one) + diag_one, same_one, block_width)
    region = jnp.concatenate(
        [
            jnp.concatenate([root_local, -solved_one], axis=1),
            jnp.concatenate([-turned_one, inverse_one], axis=1),
        ],
        axis=0,
    )
    region_gathered = lax.all_gather(to_blocks(region, block_width), "pcol", axis=4, tiled=True)
    product_part = split_rows(
        contract(row_panel(region_gathered), masked_two), prow_total, block_width
    )
    solved_two = merge_rows(lax.psum_scatter(product_part, "prow", scatter_dimension=1, tiled=True))
    diag_two_part = split_rows(contract(second_full, solved_two), prow_total, block_width)
    diag_two = merge_rows(lax.psum_scatter(diag_two_part, "prow", scatter_dimension=1, tiled=True))
    same_two = same_mask(seg_two[row_ids(dinv_two.shape[0])], seg_two[col_ids(dinv_two.shape[3])])
    inverse_two = apply_mask(flatten_local(dinv_two) + diag_two, same_two, block_width)
    return (to_blocks(inverse_one, block_width), to_blocks(inverse_two, block_width))


def solution(mesh):
    return jax.shard_map(
        on_device,
        mesh=mesh,
        in_specs=(
            P(None, "prow", None, None, "pcol", None),
            P(None, "prow", None, None, "pcol", None),
            P(None, "prow", None, None, "pcol", None),
            P(None, "prow", None, None, "pcol", None),
            P(None, "prow", None, None, "pcol", None),
            P(),
            P(),
            P(),
            P(),
            P(),
        ),
        out_specs=(
            P(None, "prow", None, None, "pcol", None),
            P(None, "prow", None, None, "pcol", None),
        ),
        check_vma=False,
    )
```

profile of v0, /device:TPU:2, one launch (start us, length us, event | category | flops | bytes accessed | tf_op | source)
XLA Modules:
  0.0 629.4 jit_solution(16628335298792741638)
XLA Ops:
  14.1 55.8 %all-gather.7.cloned.1.call-done = f32[2,1,128,2,16,128]{5,2,3,1,0,4:T(8,128)} async-done(((f32[2,1,128,2,1,128]{5,2,3,1,0,4:T(8,128)}), f32[2,1,128,2,16,128]{5,2,3,1,0,4:T(8,128)}) %all-gather.7.cloned.1.call-update) | async-done | bytes 4194320 | tf_op jit(solution)/shard_map/all_gather | solution.py:117
  70.0 6.6 %copy.54 = f32[2,1,128,2,16,128]{5,4,3,2,0,1:T(8,128)} copy(f32[2,1,128,2,16,128]{5,2,3,1,0,4:T(8,128)} %all-gather.7.cloned.1.call-done) | data formatting | bytes 8388608 | tf_op jit(solution)/shard_map/all_gather | solution.py:117
  76.6 5.0 reshape_squeeze.20
  81.6 4.5 convolution_bitcast_fusion.1
  88.7 33.1 %all-gather.5.cloned.1.call-done = f32[2,1,128,1,16,128]{5,2,3,1,0,4:T(8,128)} async-done(((f32[2,1,128,1,1,128]{5,2,3,1,0,4:T(8,128)}), f32[2,1,128,1,16,128]{5,2,3,1,0,4:T(8,128)}) %all-gather.5.cloned.1.call-update) | async-done | bytes 2097168 | tf_op jit(solution)/shard_map/all_gather | solution.py:118
  121.8 2.8 copy.51
  124.6 2.2 copy.79
  128.7 3.1 convolution_bitcast_fusion
  132.1 51.4 %reduce-scatter.8.cloned.1.call-done = f32[2,1,128,128]{3,2,0,1:T(8,128)} async-done(((f32[2,16,128,128]{3,2,0,1:T(8,128)}), f32[2,1,128,128]{3,2,0,1:T(8,128)}) %reduce-scatter.8.cloned.1.call-update) | async-done | bytes 131088 | tf_op jit(solution)/shard_map/reduce_scatter | solution.py:127
  183.4 3.8 convolution_bitcast_fusion.2
  188.6 54.9 %reduce-scatter.12.cloned.1.call-done = f32[1,1,128,256]{3,2,1,0:T(8,128)} async-done(((f32[1,16,128,256]{3,2,1,0:T(8,128)}), f32[1,1,128,256]{3,2,1,0:T(8,128)}) %reduce-scatter.12.cloned.1.call-update) | async-done | bytes 131088 | tf_op jit(solution)/shard_map/reduce_scatter | solution.py:128
  244.4 57.2 %reduce-scatter.10.cloned.1.call-done = f32[1,1,128,128]{3,2,1,0:T(8,128)} async-done(((f32[1,16,128,128]{3,2,1,0:T(8,128)}), f32[1,1,128,128]{3,2,1,0:T(8,128)}) %reduce-scatter.10.cloned.1.call-update) | async-done | bytes 65552 | tf_op jit(solution)/shard_map/reduce_scatter | solution.py:133
  310.3 72.9 %all-gather.11.cloned.1.call-done = f32[3,1,128,3,16,128]{5,2,3,1,0,4:T(8,128)} async-done(((f32[3,1,128,3,1,128]{5,2,3,1,0,4:T(8,128)}), f32[3,1,128,3,16,128]{5,2,3,1,0,4:T(8,128)}) %all-gather.11.cloned.1.call-update) | async-done | bytes 9437200 | tf_op jit(solution)/shard_map/all_gather | solution.py:143
  383.2 12.8 %copy.63 = f32[3,1,128,3,16,128]{5,4,3,2,0,1:T(8,128)} copy(f32[3,1,128,3,16,128]{5,2,3,1,0,4:T(8,128)} %all-gather.11.cloned.1.call-done) | data formatting | bytes 18874368 | tf_op jit(solution)/shard_map/all_gather | solution.py:143
  395.9 10.0 %reshape_squeeze.24 = f32[384,6144]{1,0:T(8,128)} reshape(f32[3,1,128,3,16,128]{5,4,3,2,0,1:T(8,128)} %copy.63) | data formatting | bytes 18874368 | tf_op jit(solution)/shard_map/reshape;squeeze | solution.py:58
  406.0 9.6 %copy.64 = f32[6144,384]{1,0:T(8,128)} copy(f32[6144,384]{0,1:T(8,128)} %bitcast.148) | data formatting | bytes 18874368 | tf_op jit(solution)/shard_map/dot_general | solution.py:10
  415.6 11.0 %fusion.25 = f32[3,16,128,128]{3,2,1,0:T(8,128)} fusion(f32[3,16,128,384]{3,2,1,0:T(8,128)} %bitcast.149, f32[384,128,1,1]{1,0,3,2:T(8,128)S(1)} %bitcast.160), kind=kOutput, calls=%fused_computation.60 | convolution fusion | flops 3623878656 | bytes 12779520 | tf_op jit(solution)/shard_map/dot_general | solution.py:10
  427.9 10.0 %all-gather.9.cloned.1.call-done = f32[3,1,128,1,16,128]{5,2,3,1,0,4:T(8,128)} async-done(((f32[3,1,128,1,1,128]{5,2,3,1,0,4:T(8,128)}), f32[3,1,128,1,16,128]{5,2,3,1,0,4:T(8,128)}) %all-gather.9.cloned.1.call-update) | async-done | bytes 3145744 | tf_op jit(solution)/shard_map/all_gather | solution.py:119
  437.9 3.7 copy.60
  441.6 3.1 copy.78
  444.7 2.4 copy.61
  447.1 111.4 %all-reduce.3.cloned.1.call-done = f32[3,16,128,128]{3,2,1,0:T(8,128)} async-done(((f32[3,16,128,128]{3,2,1,0:T(8,128)}), f32[3,16,128,128]{3,2,1,0:T(8,128)}) %all-reduce.3.cloned.1.call-update) | async-done | bytes 3145744
  560.1 3.7 convolution_bitcast_fusion.3
  565.6 55.8 %reduce-scatter.14.cloned.1.call-done = f32[1,1,128,128]{3,2,1,0:T(8,128)} async-done(((f32[1,16,128,128]{3,2,1,0:T(8,128)}), f32[1,1,128,128]{3,2,1,0:T(8,128)}) %reduce-scatter.14.cloned.1.call-update) | async-done | bytes 65552 | tf_op jit(solution)/shard_map/reduce_scatter | solution.py:149
  (78 shorter events, 24.5 us)
Async XLA Ops:
  7.2 62.8 %all-gather.7.cloned.1.call-start = ((), (), s32[]{:S(2)}) async-start(), calls=%async_computation.5 | async-start | bytes 4456448 | tf_op jit(solution)/shard_map/all_gather | solution.py:117
  8.9 112.9 %all-gather.5.cloned.1.call-start = ((), (), s32[]{:S(2)}) async-start(), calls=%async_computation.4 | async-start | bytes 2228224 | tf_op jit(solution)/shard_map/all_gather | solution.py:118
  14.1 169.4 %reduce-scatter.8.cloned.1.call-start = ((), (), s32[]{:S(2)}) async-start(), calls=%async_computation.6 | async-start | bytes 2228224 | tf_op jit(solution)/shard_map/reduce_scatter | solution.py:127
  76.6 5.0 copy-start.3
  86.5 2.0 copy-start.1
  88.4 155.1 %reduce-scatter.12.cloned.1.call-start = ((), (), s32[]{:S(2)}) async-start(), calls=%async_computation.9 | async-start | bytes 2228224 | tf_op jit(solution)/shard_map/reduce_scatter | solution.py:128
  131.8 169.7 %copy-start.5 = (f32[1,1,128,1,1,128]{5,4,3,2,1,0:T(1,128)S(1)}, f32[1,1,128,1,1,128]{5,4,3,2,1,0:T(1,128)}, u32[]{:S(2)}) copy-start(f32[1,1,128,1,1,128]{5,4,3,2,1,0:T(1,128)} %param.13) | copy-start | bytes 196612
  131.8 169.7 %reduce-scatter.10.cloned.1.call-start = ((), (), s32[]{:S(2)}) async-start(), calls=%async_computation.7 | async-start | bytes 1114112 | tf_op jit(solution)/shard_map/reduce_scatter | solution.py:133
  183.4 61.0 %copy-start.4 = (f32[2,1,128,128]{3,2,0,1:T(8,128)S(1)}, f32[2,1,128,128]{3,2,0,1:T(8,128)}, u32[]{:S(2)}) copy-start(f32[2,1,128,128]{3,2,0,1:T(8,128)} %reduce-scatter.8.cloned.1.call-done) | copy-start | bytes 393220
  187.2 118.2 %copy-start = (s32[16]{0:T(128)S(1)}, s32[16]{0:T(128)}, u32[]{:S(2)}) copy-start(s32[16]{0:T(128)} %param.15) | copy-start | bytes 196
  187.3 195.9 %all-gather.11.cloned.1.call-start = ((), (), s32[]{:S(2)}) async-start(), calls=%async_computation.10 | async-start | bytes 10027008 | tf_op jit(solution)/shard_map/all_gather | solution.py:143
  188.5 117.5 %copy-start.9 = (s32[4,48]{1,0:T(4,128)S(1)}, s32[4,48]{1,0:T(4,128)}, u32[]{:S(2)}) copy-start(s32[4,48]{1,0:T(4,128)} %param.19) | copy-start | bytes 2308
  188.5 118.2 %copy-start.10 = (s32[4]{0:T(128)S(1)}, s32[4]{0:T(128)}, u32[]{:S(2)}) copy-start(s32[4]{0:T(128)} %param.17) | copy-start | bytes 52
  188.6 120.9 %copy-start.7 = (f32[3,1,128,1,1,128]{5,4,3,2,1,0:T(1,128)S(1)}, f32[3,1,128,1,1,128]{5,4,3,2,1,0:T(1,128)}, u32[]{:S(2)}) copy-start(f32[3,1,128,1,1,128]{5,4,3,2,1,0:T(1,128)} %param.12) | copy-start | bytes 589828
  303.6 134.3 %all-gather.9.cloned.1.call-start = ((), (), s32[]{:S(2)}) async-start(), calls=%async_computation.8 | async-start | bytes 3342336 | tf_op jit(solution)/shard_map/all_gather | solution.py:119
  310.2 248.3 %all-reduce.3.cloned.1.call-start = ((), (), s32[]{:S(2)}) async-start(), calls=%async_computation.12 | async-start | bytes 6291456
  406.0 9.6 %copy-start.2 = (f32[3,1,128,1,1,128]{5,2,3,1,0,4:T(8,128)S(1)}, f32[3,1,128,1,1,128]{5,2,3,1,0,4:T(8,128)}, u32[]{:S(2)}) copy-start(f32[3,1,128,1,1,128]{5,2,3,1,0,4:T(8,128)} %broadcast_multiply_fusion) | copy-start | bytes 589828
  426.6 0.7 copy-start.11
  426.6 194.8 %reduce-scatter.14.cloned.1.call-start = ((), (), s32[]{:S(2)}) async-start(), calls=%async_computation.11 | async-start | bytes 1114112 | tf_op jit(solution)/shard_map/reduce_scatter | solution.py:149
  447.1 117.9 %copy-start.6 = (f32[1,1,128,128]{3,2,1,0:T(8,128)S(1)}, f32[1,1,128,128]{3,2,1,0:T(8,128)}, u32[]{:S(2)}) copy-start(f32[1,1,128,128]{3,2,1,0:T(8,128)} %reduce-scatter.10.cloned.1.call-done) | copy-start | bytes 196612
  447.1 174.3 %copy-start.8 = (f32[1,1,128,1,1,128]{5,4,3,2,1,0:T(1,128)S(1)}, f32[1,1,128,1,1,128]{5,4,3,2,1,0:T(1,128)}, u32[]{:S(2)}) copy-start(f32[1,1,128,1,1,128]{5,4,3,2,1,0:T(1,128)} %param.14) | copy-start | bytes 196612
Sparse Core Ops, SparseCore 0:
  10.4 59.4 all-gather.6
  72.4 49.3 all-gather.4
  124.3 59.0 reduce-scatter.7
  185.8 57.5 reduce-scatter.11
  245.8 55.7 reduce-scatter.9
  304.1 78.9 all-gather.10
  385.9 51.9 all-gather.8
  440.4 118.0 all-reduce.2
  564.0 57.4 reduce-scatter.13
where the time goes:
time: 630 us; the launch traced here: 629 us
  waiting for transfers between devices  503 us (80%)
  local copies, waits for them, and re-layouts  73.2 us (12%)
  matrix products  28.3 us (4%)
  between operations  18.2 us (3%)
  other arithmetic  6.39 us (1%)
    unnamed x10, waiting for transfers between devices  112 us
    all_gather x1, waiting for transfers between devices, on_device(): lax.all_gather(to_blocks(region, block_width), 'pcol', axis=4, tiled=True)  72.9 us
    reduce_scatter x1, waiting for transfers between devices, on_device(): lax.psum_scatter(diag_part, 'prow', scatter_dimension=1, tiled=True)  57.2 us
    all_gather x1, waiting for transfers between devices, on_device(): lax.all_gather(root_inverse, 'pcol', axis=4, tiled=True)  55.8 us
    reduce_scatter x1, waiting for transfers between devices, on_device(): lax.psum_scatter(diag_two_part, 'prow', scatter_dimension=1, tiled=True)  55.8 us
    reduce_scatter x1, waiting for transfers between devices, on_device(): lax.psum_scatter(turned_part, 'prow', scatter_dimension=1, tiled=True)  54.9 us
    reduce_scatter x1, waiting for transfers between devices, on_device(): lax.psum_scatter(solved_part, 'prow', scatter_dimension=1, tiled=True)  51.4 us
    all_gather x1, waiting for transfers between devices, on_device(): lax.all_gather(to_blocks(masked_one, block_width), 'pcol', axis=4, tiled=...  33.1 us
  transfers between devices with their start and end apart: 9, of which 9 were waited for; matrix products, arithmetic and copies ran while one was open for 15% of the time, Pallas kernels for 0%

commit v1 on v0

--- a/solution.py
+++ b/solution.py
@@ -140,7 +140,12 @@
         ],
         axis=0,
     )
-    region_gathered = lax.all_gather(to_blocks(region, block_width), "pcol", axis=4, tiled=True)
+    region_gathered = jnp.concatenate(
+        lax.all_to_all(
+            jnp.stack([to_blocks(region, block_width)] * lax.axis_size("pcol")), "pcol", 0, 0
+        ),
+        axis=4,
+    )
     product_part = split_rows(
         contract(row_panel(region_gathered), masked_two), prow_total, block_width
     )

time: 630 us -> 700 us (1.11)
  waiting for transfers between devices: 503 us -> 560 us
  starting transfers between devices: 0.77 us -> 8.13 us
    all_to_all x0 -> x1, waiting for transfers between devices: none -> 138 us  [on_device(): lax.all_to_all(jnp.stack([to_blocks(region, block_width)] * lax.axis_size...]
    all_gather x1 -> x0, waiting for transfers between devices: 72.9 us -> none  [on_device(): lax.all_gather(to_blocks(region, block_width), 'pcol', axis=4, tiled=True)]
    all_gather x1 -> x0, local copies, waits for them, and re-layouts: 12.8 us -> none  [on_device(): lax.all_gather(to_blocks(region, block_width), 'pcol', axis=4, tiled=True)]
    reshape x2 -> x1, local copies, waits for them, and re-layouts: 1.1 us -> 12.8 us  [on_device(): jnp.concatenate(lax.all_to_all(jnp.stack([to_blocks(region, block_width)]...]
    all_gather x1, waiting for transfers between devices: 10 us -> 0.01 us  [on_device(): lax.all_gather(to_blocks(masked_two, block_width), 'pcol', axis=4, tiled=...]
    all_to_all x0 -> x1, starting transfers between devices: none -> 7.4 us  [on_device(): lax.all_to_all(jnp.stack([to_blocks(region, block_width)] * lax.axis_size...]
    unnamed x10 -> x9, waiting for transfers between devices: 112 us -> 114 us
  transfers between devices with their start and end apart: 9 -> 9, of which waited for: 9 -> 8; matrix products, arithmetic and copies ran while one was open for 15% -> 14% of each run, Pallas kernels for 0% -> 0%
where the time goes in v1:
time: 700 us; the launch traced here: 699 us
  waiting for transfers between devices  560 us (80%)
  local copies, waits for them, and re-layouts  77.1 us (11%)
  matrix products  28.4 us (4%)
  between operations  18.6 us (3%)
  starting transfers between devices  8.13 us (1%)
    all_to_all x1, waiting for transfers between devices, on_device(): lax.all_to_all(jnp.stack([to_blocks(region, block_width)] * lax.axis_size...  138 us
    unnamed x9, waiting for transfers between devices  114 us
    reduce_scatter x1, waiting for transfers between devices, on_device(): lax.psum_scatter(diag_part, 'prow', scatter_dimension=1, tiled=True)  57.2 us
    reduce_scatter x1, waiting for transfers between devices, on_device(): lax.psum_scatter(diag_two_part, 'prow', scatter_dimension=1, tiled=True)  55.7 us
    all_gather x1, waiting for transfers between devices, on_device(): lax.all_gather(root_inverse, 'pcol', axis=4, tiled=True)  55.7 us
    reduce_scatter x1, waiting for transfers between devices, on_device(): lax.psum_scatter(turned_part, 'prow', scatter_dimension=1, tiled=True)  54.9 us
    reduce_scatter x1, waiting for transfers between devices, on_device(): lax.psum_scatter(solved_part, 'prow', scatter_dimension=1, tiled=True)  51.3 us
    all_gather x1, waiting for transfers between devices, on_device(): lax.all_gather(to_blocks(masked_one, block_width), 'pcol', axis=4, tiled=...  33.1 us
  transfers between devices with their start and end apart: 9, of which 8 were waited for; matrix products, arithmetic and copies ran while one was open for 14% of the time, Pallas kernels for 0%

profile of v1, /device:TPU:2, one launch (start us, length us, event | category | flops | bytes accessed | tf_op | source)
XLA Modules:
  0.0 698.9 jit_solution(5657802204680895293)
XLA Ops:
  14.2 55.7 %all-gather.6.cloned.1.call-done = f32[2,1,128,2,16,128]{5,2,3,1,0,4:T(8,128)} async-done(((f32[2,1,128,2,1,128]{5,2,3,1,0,4:T(8,128)}), f32[2,1,128,2,16,128]{5,2,3,1,0,4:T(8,128)}) %all-gather.6.cloned.1.call-update) | async-done | bytes 4194320 | tf_op jit(solution)/shard_map/all_gather | solution.py:117
  70.0 6.6 copy.70
  76.6 5.0 reshape_squeeze.17
  81.6 4.5 convolution_bitcast_fusion.1
  88.7 33.1 %all-gather.4.cloned.1.call-done = f32[2,1,128,1,16,128]{5,2,3,1,0,4:T(8,128)} async-done(((f32[2,1,128,1,1,128]{5,2,3,1,0,4:T(8,128)}), f32[2,1,128,1,16,128]{5,2,3,1,0,4:T(8,128)}) %all-gather.4.cloned.1.call-update) | async-done | bytes 2097168 | tf_op jit(solution)/shard_map/all_gather | solution.py:118
  121.8 2.8 copy.67
  128.7 3.1 convolution_bitcast_fusion
  132.1 51.3 %reduce-scatter.8.cloned.1.call-done = f32[2,1,128,128]{3,2,0,1:T(8,128)} async-done(((f32[2,16,128,128]{3,2,0,1:T(8,128)}), f32[2,1,128,128]{3,2,0,1:T(8,128)}) %reduce-scatter.8.cloned.1.call-update) | async-done | bytes 131088 | tf_op jit(solution)/shard_map/reduce_scatter | solution.py:127
  183.4 3.8 convolution_bitcast_fusion.2
  188.5 54.9 %reduce-scatter.12.cloned.1.call-done = f32[1,1,128,256]{3,2,1,0:T(8,128)} async-done(((f32[1,16,128,256]{3,2,1,0:T(8,128)}), f32[1,1,128,256]{3,2,1,0:T(8,128)}) %reduce-scatter.12.cloned.1.call-update) | async-done | bytes 131088 | tf_op jit(solution)/shard_map/reduce_scatter | solution.py:128
  244.4 57.2 %reduce-scatter.10.cloned.1.call-done = f32[1,1,128,128]{3,2,1,0:T(8,128)} async-done(((f32[1,16,128,128]{3,2,1,0:T(8,128)}), f32[1,1,128,128]{3,2,1,0:T(8,128)}) %reduce-scatter.10.cloned.1.call-update) | async-done | bytes 65552 | tf_op jit(solution)/shard_map/reduce_scatter | solution.py:133
  302.8 4.8 stack.3
  307.6 7.4 %all-to-all-start = ((f32[16,3,1,128,3,1,128]{6,3,5,4,2,1,0:T(8,128)}), f32[16,3,1,128,3,1,128]{6,3,5,4,2,1,0:T(8,128)}, u32[]{:S(2)}, u32[]{:S(2)}) async-start(f32[16,3,1,128,3,1,128]{6,3,5,4,2,1,0:T(8,128)} %stack.3), calls=%async_computation.3 | async-start | bytes 18874368 | tf_op jit(solution)/shard_map/all_to_all | solution.py:144
  321.6 138.2 %all-to-all-done = f32[16,3,1,128,3,1,128]{6,3,5,4,2,1,0:T(8,128)} async-done(((f32[16,3,1,128,3,1,128]{6,3,5,4,2,1,0:T(8,128)}), f32[16,3,1,128,3,1,128]{6,3,5,4,2,1,0:T(8,128)}, u32[]{:S(2)}, u32[]{:S(2)}) %all-to-all-start) | async-done | bytes 9437216 | tf_op jit(solution)/shard_map/all_to_all | solution.py:144
  459.8 12.8 %copy.79 = f32[3,1,128,3,16,1,128]{6,4,3,2,0,5,1:T(8,128)} copy(f32[3,1,128,3,16,1,128]{6,2,5,3,1,0,4:T(8,128)} %bitcast.41) | data formatting | bytes 18874368 | tf_op jit(solution)/shard_map/reshape | solution.py:143
  472.5 10.0 %reshape_squeeze_reshape.3 = f32[384,6144]{1,0:T(8,128)} reshape(f32[3,1,128,3,16,1,128]{6,4,3,2,0,5,1:T(8,128)} %copy.79) | data formatting | bytes 18874368 | tf_op jit(solution)/shard_map/reshape;squeeze;reshape | solution.py:58
  482.5 9.6 %copy.80 = f32[6144,384]{1,0:T(8,128)} copy(f32[6144,384]{0,1:T(8,128)} %bitcast.149) | data formatting | bytes 18874368 | tf_op jit(solution)/shard_map/dot_general | solution.py:10
  492.1 11.0 %fusion.25 = f32[3,16,128,128]{3,2,1,0:T(8,128)} fusion(f32[3,16,128,384]{3,2,1,0:T(8,128)} %bitcast.150, f32[384,128,1,1]{1,0,3,2:T(8,128)S(1)} %bitcast.161), kind=kOutput, calls=%fused_computation.60 | convolution fusion | flops 3623878656 | bytes 12779520 | tf_op jit(solution)/shard_map/dot_general | solution.py:10
  504.4 3.7 copy.76
  508.1 3.2 copy.94
  511.3 2.4 copy.77
  513.7 114.0 %all-reduce.3.cloned.1.call-done = f32[3,16,128,128]{3,2,1,0:T(8,128)} async-done(((f32[3,16,128,128]{3,2,1,0:T(8,128)}), f32[3,16,128,128]{3,2,1,0:T(8,128)}) %all-reduce.3.cloned.1.call-update) | async-done | bytes 3145744
  629.3 3.7 convolution_bitcast_fusion.3
  634.9 55.7 %reduce-scatter.14.cloned.1.call-done = f32[1,1,128,128]{3,2,1,0:T(8,128)} async-done(((f32[1,16,128,128]{3,2,1,0:T(8,128)}), f32[1,1,128,128]{3,2,1,0:T(8,128)}) %reduce-scatter.14.cloned.1.call-update) | async-done | bytes 65552 | tf_op jit(solution)/shard_map/reduce_scatter | solution.py:154
  (78 shorter events, 25.8 us)
Async XLA Ops:
  7.2 62.8 %all-gather.6.cloned.1.call-start = ((), (), s32[]{:S(2)}) async-start(), calls=%async_computation.6 | async-start | bytes 4456448 | tf_op jit(solution)/shard_map/all_gather | solution.py:117
  8.9 112.9 %all-gather.4.cloned.1.call-start = ((), (), s32[]{:S(2)}) async-start(), calls=%async_computation.5 | async-start | bytes 2228224 | tf_op jit(solution)/shard_map/all_gather | solution.py:118
  14.2 169.3 %reduce-scatter.8.cloned.1.call-start = ((), (), s32[]{:S(2)}) async-start(), calls=%async_computation.7 | async-start | bytes 2228224 | tf_op jit(solution)/shard_map/reduce_scatter | solution.py:127
  76.6 5.0 copy-start.3
  86.5 2.0 copy-start.1
  88.4 155.1 %reduce-scatter.12.cloned.1.call-start = ((), (), s32[]{:S(2)}) async-start(), calls=%async_computation.10 | async-start | bytes 2228224 | tf_op jit(solution)/shard_map/reduce_scatter | solution.py:128
  131.8 169.7 %copy-start.5 = (f32[1,1,128,1,1,128]{5,4,3,2,1,0:T(1,128)S(1)}, f32[1,1,128,1,1,128]{5,4,3,2,1,0:T(1,128)}, u32[]{:S(2)}) copy-start(f32[1,1,128,1,1,128]{5,4,3,2,1,0:T(1,128)} %param.13) | copy-start | bytes 196612
  131.8 169.7 %reduce-scatter.10.cloned.1.call-start = ((), (), s32[]{:S(2)}) async-start(), calls=%async_computation.8 | async-start | bytes 1114112 | tf_op jit(solution)/shard_map/reduce_scatter | solution.py:133
  183.4 61.0 %copy-start.4 = (f32[2,1,128,128]{3,2,0,1:T(8,128)S(1)}, f32[2,1,128,128]{3,2,0,1:T(8,128)}, u32[]{:S(2)}) copy-start(f32[2,1,128,128]{3,2,0,1:T(8,128)} %reduce-scatter.8.cloned.1.call-done) | copy-start | bytes 393220
  307.6 9.2 %copy-start = (s32[16]{0:T(128)S(1)}, s32[16]{0:T(128)}, u32[]{:S(2)}) copy-start(s32[16]{0:T(128)} %param.15) | copy-start | bytes 196
  307.6 9.9 %copy-start.9 = (s32[4,48]{1,0:T(4,128)S(1)}, s32[4,48]{1,0:T(4,128)}, u32[]{:S(2)}) copy-start(s32[4,48]{1,0:T(4,128)} %param.19) | copy-start | bytes 2308
  307.6 10.5 %copy-start.10 = (s32[4]{0:T(128)S(1)}, s32[4]{0:T(128)}, u32[]{:S(2)}) copy-start(s32[4]{0:T(128)} %param.17) | copy-start | bytes 52
  307.6 13.1 %copy-start.7 = (f32[3,1,128,1,1,128]{5,4,3,2,1,0:T(1,128)S(1)}, f32[3,1,128,1,1,128]{5,4,3,2,1,0:T(1,128)}, u32[]{:S(2)}) copy-start(f32[3,1,128,1,1,128]{5,4,3,2,1,0:T(1,128)} %param.12) | copy-start | bytes 589828
  307.6 152.2 %all-to-all-start = ((f32[16,3,1,128,3,1,128]{6,3,5,4,2,1,0:T(8,128)}), f32[16,3,1,128,3,1,128]{6,3,5,4,2,1,0:T(8,128)}, u32[]{:S(2)}, u32[]{:S(2)}) async-start(f32[16,3,1,128,3,1,128]{6,3,5,4,2,1,0:T(8,128)} %stack.3), calls=%async_computation.3 | async-start | bytes 18874368 | tf_op jit(solution)/shard_map/all_to_all | solution.py:144
  315.0 189.4 %all-gather.8.cloned.1.call-start = ((), (), s32[]{:S(2)}) async-start(), calls=%async_computation.9 | async-start | bytes 3342336 | tf_op jit(solution)/shard_map/all_gather | solution.py:119
  321.5 306.2 %all-reduce.3.cloned.1.call-start = ((), (), s32[]{:S(2)}) async-start(), calls=%async_computation.12 | async-start | bytes 6291456
  482.5 9.6 %copy-start.2 = (f32[3,1,128,1,1,128]{5,2,3,1,0,4:T(8,128)S(1)}, f32[3,1,128,1,1,128]{5,2,3,1,0,4:T(8,128)}, u32[]{:S(2)}) copy-start(f32[3,1,128,1,1,128]{5,2,3,1,0,4:T(8,128)} %broadcast_multiply_fusion) | copy-start | bytes 589828
  503.1 0.7 copy-start.11
  503.2 187.4 %reduce-scatter.14.cloned.1.call-start = ((), (), s32[]{:S(2)}) async-start(), calls=%async_computation.11 | async-start | bytes 1114112 | tf_op jit(solution)/shard_map/reduce_scatter | solution.py:154
  513.7 120.6 %copy-start.6 = (f32[1,1,128,128]{3,2,1,0:T(8,128)S(1)}, f32[1,1,128,128]{3,2,1,0:T(8,128)}, u32[]{:S(2)}) copy-start(f32[1,1,128,128]{3,2,1,0:T(8,128)} %reduce-scatter.10.cloned.1.call-done) | copy-start | bytes 196612
  513.7 176.9 %copy-start.8 = (f32[1,1,128,1,1,128]{5,4,3,2,1,0:T(1,128)S(1)}, f32[1,1,128,1,1,128]{5,4,3,2,1,0:T(1,128)}, u32[]{:S(2)}) copy-start(f32[1,1,128,1,1,128]{5,4,3,2,1,0:T(1,128)} %param.14) | copy-start | bytes 196612
Sparse Core Ops, SparseCore 0:
  10.4 59.4 all-gather.5
  72.4 49.3 all-gather.3
  124.3 59.0 reduce-scatter.7
  185.8 57.5 reduce-scatter.11
  245.8 55.7 reduce-scatter.9
  321.6 136.1 all-gather.7
  503.3 124.3 all-reduce.2
  633.1 57.4 reduce-scatter.13
